TPU v7x, 32 devices: a whole 2x2x4 slice. The times are simulated.
32 devices in a mesh: tile: 8 (over y, x, core), depth: 4 (over z).
Axes of the slice: x: 2, y: 2, z: 4, core: 2. Of those that a mesh axis runs over, the one named last changes fastest.
Arguments:
- features: bfloat16 [4, 2048, 128], P('depth', 'tile'), may hold values from -4 to 4
- logits: float32 [4, 2048], P('depth', 'tile'), may hold values from -2.75 to 5.5
- geometry: float32 [2, 4, 5, 2048], P(None, 'depth', None, 'tile'), may hold values from -0.6 to 32, as said below
- dest_slot: int32 [2, 4, 2048], P(None, 'depth', 'tile'), may hold values from -1 to 2047, as said below
- target: bfloat16 [2, 16, 128, 1024], P(None, 'tile'), may hold values from -3 to 3
Outputs:
- images: bfloat16 [2, 16, 128, 1024], P(None, 'tile', None, 'depth')
- new_features: bfloat16 [4, 2048, 128], P('depth', 'tile')
- new_logits: float32 [4, 2048], P('depth', 'tile')
- shape_grads: float32 [2, 4, 5, 2048], P(None, 'depth', None, 'tile')
Inputs may be any that keep to these rules, and one draw needn't show every extreme that they name: `dest_slot`: for each view and layer no two splats share a slot; -1 marks a splat outside the view; a splat's place within its tile is its front-to-back order. At most 32 splats of one layer held by one index of tile go to the tiles of one index of tile, and in every view and layer there is an index of tile whose tiles receive exactly 32 from every owner, so that all their slots are used. `geometry`: components 0 and 1 are a splat's centre in pixels within its tile, from 0 to 32; components 2 and 3 lie in -0.5 to 2.0; component 4 in -0.6 to 0.6.
All inputs are finite; a program needn't handle non-finite values.
Results may differ from a plain program's by a relative error of at most 0.0073.
Values may be sent and summed in bfloat16 or wider, within the bound.
A program may use at most 64 MiB of HBM per device.

v0:
```python
from functools import partial
import jax
import jax.numpy as jnp
from jax import lax
from jax.sharding import PartitionSpec as P

F = 128
W = 32
S = 128
VIEWS = 2
P_SIZE = 1024
clamp_top = 0.99
feature_rate = 0.5
opacity_rate = 0.5


def pixel_places():
    places = jnp.arange(P_SIZE, dtype=jnp.int32)
    across = (places % W).astype(jnp.float32) + 0.5
    downward = (places // W).astype(jnp.float32) + 0.5
    return (across, downward)


def block_sum(values, reverse):
    length = values.shape[0]
    block_rows = min(128, length)
    blocks = values.reshape(length // block_rows, block_rows, values.shape[1])
    positions = jnp.arange(block_rows)
    if reverse:
        triangle = (positions[:, None] < positions[None, :]).astype(jnp.float32)
    else:
        triangle = (positions[:, None] > positions[None, :]).astype(jnp.float32)
    within = jnp.einsum("ij,bjp->bip", triangle, blocks, precision=lax.Precision.HIGHEST)
    block_totals = jnp.sum(blocks, axis=1)
    if reverse:
        offsets = jnp.sum(block_totals, axis=0)[None, :] - jnp.cumsum(block_totals, axis=0)
    else:
        offsets = jnp.cumsum(block_totals, axis=0) - block_totals
    return (within + offsets[:, None, :]).reshape(length, values.shape[1])


def splat_fields(shapes):
    across, downward = pixel_places()
    delta_x = across[None, :] - shapes[0][:, None]
    delta_y = downward[None, :] - shapes[1][:, None]
    coef_a = jnp.exp(shapes[2])[:, None]
    coef_c = jnp.exp(shapes[3])[:, None]
    spread = jnp.exp(0.5 * (shapes[2] + shapes[3]))[:, None]
    coef_b = shapes[4][:, None] * spread
    quadric = (
        coef_a * delta_x * delta_x + 2.0 * coef_b * delta_x * delta_y + coef_c * delta_y * delta_y
    )
    falloff = jnp.exp(-0.5 * quadric)
    opacity = shapes[5][:, None]
    product = opacity * falloff
    coverage = jnp.minimum(product, clamp_top)
    return (delta_x, delta_y, coef_a, coef_b, coef_c, spread, falloff, opacity, product, coverage)


def layer_forward(inputs):
    slot_feats, shapes = inputs
    coverage = splat_fields(shapes)[9]
    log_keep = jnp.log(1.0 - coverage)
    before = block_sum(log_keep, False)
    weights = (coverage * jnp.exp(before)).astype(jnp.bfloat16)
    composite = lax.dot_general(
        slot_feats, weights, (((0,), (0,)), ((), ())), preferred_element_type=jnp.float32
    )
    layer_keep = jnp.exp(jnp.sum(log_keep, axis=0))
    return (composite, layer_keep)


def layer_backward(inputs):
    slot_feats, shapes, grad_comp, grad_keep = inputs
    delta_x, delta_y, coef_a, coef_b, coef_c, spread, falloff, opacity, product, coverage = (
        splat_fields(shapes)
    )
    log_keep = jnp.log(1.0 - coverage)
    before = block_sum(log_keep, False)
    decayed = jnp.exp(before)
    exact_weight = coverage * decayed
    weights = exact_weight.astype(jnp.bfloat16)
    layer_keep = jnp.exp(jnp.sum(log_keep, axis=0))
    grad_feat = lax.dot_general(
        weights, grad_comp, (((1,), (1,)), ((), ())), preferred_element_type=jnp.float32
    )
    grad_weight = jnp.dot(slot_feats, grad_comp, preferred_element_type=jnp.float32)
    grad_before = grad_weight * exact_weight
    later = block_sum(grad_before, True)
    grad_log = later + (grad_keep * layer_keep)[None, :]
    grad_coverage = grad_weight * decayed - grad_log / (1.0 - coverage)
    grad_product = jnp.where(product < clamp_top, grad_coverage, 0.0)
    grad_quadric = -0.5 * opacity * falloff * grad_product
    grad_mean_x = -2.0 * jnp.sum(grad_quadric * (coef_a * delta_x + coef_b * delta_y), axis=1)
    grad_mean_y = -2.0 * jnp.sum(grad_quadric * (coef_b * delta_x + coef_c * delta_y), axis=1)
    grad_first = jnp.sum(grad_quadric * delta_x * delta_x, axis=1)
    grad_cross = jnp.sum(grad_quadric * 2.0 * delta_x * delta_y, axis=1)
    grad_second = jnp.sum(grad_quadric * delta_y * delta_y, axis=1)
    grad_log_a = coef_a[:, 0] * grad_first + 0.5 * coef_b[:, 0] * grad_cross
    grad_log_c = coef_c[:, 0] * grad_second + 0.5 * coef_b[:, 0] * grad_cross
    grad_corr = spread[:, 0] * grad_cross
    opacity_flat = opacity[:, 0]
    grad_logit = opacity_flat * (1.0 - opacity_flat) * jnp.sum(falloff * grad_product, axis=1)
    grad_shape = jnp.stack(
        [grad_mean_x, grad_mean_y, grad_log_a, grad_log_c, grad_corr, grad_logit]
    )
    return (grad_feat, grad_shape)


def rear_step(all_keeps, all_terms, depth_here, layers, counter, carried):
    layer_at = layers - 1 - counter
    updated = all_terms[layer_at] + all_keeps[layer_at] * carried
    return jnp.where(layer_at > depth_here, updated, carried)


def body(features, logits, geometry, dest_slot, target):
    owners = lax.axis_size("tile")
    layers = lax.axis_size("depth")
    depth_here = lax.axis_index("depth")
    tiles_here = target.shape[1]
    owned = features.shape[1]
    capacity = owned // owners
    pixel_share = P_SIZE // layers
    splat_feats = features[0]
    logit_now = logits[0]
    images = []
    shape_grads = []
    for view_index in range(VIEWS):
        slot_ids = dest_slot[view_index, 0]
        visible = slot_ids >= 0
        receiver = jnp.where(visible, slot_ids // owned, owners)
        matches = (receiver[:, None] == jnp.arange(owners, dtype=jnp.int32)[None, :]).astype(
            jnp.int32
        )
        place_in = jnp.sum((jnp.cumsum(matches, axis=0) - matches) * matches, axis=1)
        position = jnp.where(visible, receiver * capacity + place_in, owners * capacity)
        local_slot = jnp.where(visible, slot_ids - receiver * owned, -1)
        opacity = jax.nn.sigmoid(logit_now)
        shape_rows = jnp.concatenate([geometry[view_index, 0], opacity[None, :]], axis=0).T
        row_buffer = (
            jnp.zeros((owners * capacity + 1, F), jnp.bfloat16)
            .at[position]
            .set(splat_feats)[:-1]
            .reshape(owners, capacity, F)
        )
        slot_buffer = (
            jnp.full((owners * capacity + 1,), -1, jnp.int32)
            .at[position]
            .set(local_slot)[:-1]
            .reshape(owners, capacity)
        )
        shape_buffer = (
            jnp.zeros((owners * capacity + 1, 6), jnp.float32)
            .at[position]
            .set(shape_rows)[:-1]
            .reshape(owners, capacity, 6)
        )
        got_rows, got_slots = (
            lax.all_to_all(row_buffer, "tile", split_axis=0, concat_axis=0, tiled=True),
            lax.all_to_all(slot_buffer, "tile", split_axis=0, concat_axis=0, tiled=True),
        )
        got_shapes = lax.all_to_all(shape_buffer, "tile", split_axis=0, concat_axis=0, tiled=True)
        arrived = got_slots.reshape(-1)
        present = arrived >= 0
        landing = jnp.where(present, arrived, owned)
        slot_feats = (
            jnp.zeros((owned + 1, F), jnp.bfloat16)
            .at[landing]
            .set(got_rows.reshape(-1, F))[:-1]
            .reshape(tiles_here, S, F)
        )
        slot_shapes = (
            jnp.zeros((owned + 1, 6), jnp.float32)
            .at[landing]
            .set(got_shapes.reshape(-1, 6))[:-1]
            .reshape(tiles_here, S, 6)
            .transpose(0, 2, 1)
        )
        composites, layer_keeps = lax.map(layer_forward, (slot_feats, slot_shapes))
        all_keeps = lax.all_gather(layer_keeps[None], "depth", axis=0, tiled=True)
        earlier_mask = (jnp.arange(layers) < depth_here)[:, None, None]
        ahead = jnp.prod(jnp.where(earlier_mask, all_keeps, 1.0), axis=0)
        contrib = ahead[:, None, :] * composites
        summed = lax.psum(contrib, "depth")
        residual = summed - target[view_index].astype(jnp.float32)
        image_part = lax.dynamic_slice_in_dim(summed, depth_here * pixel_share, pixel_share, 2)
        images.append(image_part.astype(jnp.bfloat16))
        pixel_terms = jnp.sum(residual * composites, axis=1)
        all_terms = lax.all_gather(pixel_terms[None], "depth", axis=0, tiled=True)
        behind = lax.fori_loop(
            0,
            layers,
            partial(rear_step, all_keeps, all_terms, depth_here, layers),
            jnp.zeros_like(pixel_terms),
        )
        grad_keep = ahead * behind
        grad_comp = (ahead[:, None, :] * residual).astype(jnp.bfloat16)
        grad_feat, grad_shape = lax.map(
            layer_backward, (slot_feats, slot_shapes, grad_comp, grad_keep)
        )
        flat_feat = grad_feat.reshape(owned, F)
        flat_shape = grad_shape.transpose(0, 2, 1).reshape(owned, 6)
        fetched = jnp.where(present, arrived, 0)
        back_feat = jnp.where(present[:, None], flat_feat[fetched], 0.0).reshape(
            owners, capacity, F
        )
        back_shape = jnp.where(present[:, None], flat_shape[fetched], 0.0).reshape(
            owners, capacity, 6
        )
        return_feat, return_shape = (
            lax.all_to_all(back_feat, "tile", split_axis=0, concat_axis=0, tiled=True),
            lax.all_to_all(back_shape, "tile", split_axis=0, concat_axis=0, tiled=True),
        )
        padded_feat = jnp.concatenate(
            [return_feat.reshape(-1, F), jnp.zeros((1, F), jnp.float32)], axis=0
        )
        padded_shape = jnp.concatenate(
            [return_shape.reshape(-1, 6), jnp.zeros((1, 6), jnp.float32)], axis=0
        )
        splat_grad_feat = padded_feat[position]
        splat_grad_shape = padded_shape[position]
        shape_grads.append(splat_grad_shape[:, :5].T)
        splat_feats = (splat_feats.astype(jnp.float32) - feature_rate * splat_grad_feat).astype(
            jnp.bfloat16
        )
        logit_now = logit_now - opacity_rate * splat_grad_shape[:, 5]
    return (jnp.stack(images), splat_feats[None], logit_now[None], jnp.stack(shape_grads)[:, None])


def solution(mesh):
    placed = (
        P("depth", "tile", None),
        P("depth", "tile"),
        P(None, "depth", None, "tile"),
        P(None, "depth", "tile"),
        P(None, "tile", None, None),
    )
    return jax.shard_map(
        body,
        mesh=mesh,
        in_specs=placed,
        out_specs=(
            P(None, "tile", None, "depth"),
            P("depth", "tile", None),
            P("depth", "tile"),
            P(None, "depth", None, "tile"),
        ),
        check_vma=False,
    )
```

profile of v0, /device:TPU:0, one launch (start us, length us, event | category | flops | bytes accessed | tf_op | source)
XLA Modules:
  0.0 308.5 jit_solution(4619955164635074478)
XLA Ops:
  15.1 5.3 %all-to-all-start = ((s32[8,1,32]{2,1,0:T(1,128)}), s32[8,1,32]{2,1,0:T(1,128)S(1)}, u32[]{:S(2)}, u32[]{:S(2)}) async-start(s32[8,1,32]{2,1,0:T(1,128)} %all_to_all.36), calls=%async_computation | async-start | bytes 8192 | tf_op jit(solution)/shard_map/all_to_all | solution.py:160
  25.1 3.3 %all-to-all-start.2 = ((f32[8,1,192]{2,1,0:T(1,128)}), f32[8,1,192]{2,1,0:T(1,128)S(1)}, u32[]{:S(2)}, u32[]{:S(2)}) async-start(f32[8,1,192]{2,1,0:T(1,128)} %reshape.3803), calls=%async_computation.2 | async-start | bytes 16384 | tf_op jit(solution)/shard_map/all_to_all | solution.py:162
  33.1 3.4 %all-to-all-start.1 = ((bf16[8,32,128]{2,1,0:T(8,128)(2,1)}), bf16[8,32,128]{2,1,0:T(8,128)(2,1)S(1)}, u32[]{:S(2)}, u32[]{:S(2)}) async-start(bf16[8,32,128]{2,1,0:T(8,128)(2,1)} %bitcast.95), calls=%async_computation.1 | async-start | bytes 131072 | tf_op jit(solution)/shard_map/all_to_all | solution.py:159
  44.0 5.1 %while.88 = (s32[]{:T(128)}, f32[2,128,1024]{2,1,0:T(8,128)S(1)}, f32[2,1024]{1,0:T(2,128)S(1)}, bf16[2,128,128]{2,1,0:T(8,128)(2,1)S(1)}, f32[2,6,128]{2,1,0:T(8,128)S(1)}, /*index=5*/s32[]{:T(128)}, s32[]{:T(128)}) while((s32[]{:T(128)}, f32[2,128,1024]{2,1,0:T(8,128)S(1)}, f32[2,1024]{1,0:T(2,128)S(1)}, ...), condition=%wide.region_11.12_spmd, body=%wide.region_8.11_spmd.sunk | while | flops 242777600 | bytes 1177693 | solution.py:179
  49.1 13.4 %all-gather.4 = f32[4,2,1024]{2,1,0:T(2,128)S(1)} all-gather(f32[1,2,1024]{2,1,0:T(2,128)S(1)} %bitcast.689), channel_id=2, replica_groups=mesh['tile'=8,'depth'=4] {'depth'}, dimensions={0}, use_global_device_ids=true | all-gather | bytes 40960 | tf_op jit(solution)/shard_map/all_gather | solution.py:180
  65.9 49.1 %all-reduce.7.cloned.1.call-done = f32[2,128,1024]{2,1,0:T(8,128)} async-done(((f32[2,128,1024]{2,1,0:T(8,128)}), f32[2,128,1024]{2,1,0:T(8,128)}) %all-reduce.7.cloned.1.call-update) | async-done | bytes 1048592 | tf_op jit(solution)/shard_map/psum | solution.py:184
  116.5 13.3 %all-gather.5 = f32[4,2,1024]{2,1,0:T(2,128)S(1)} all-gather(f32[1,2,1024]{2,1,0:T(2,128)S(1)} %bitcast.687), channel_id=3, replica_groups=mesh['tile'=8,'depth'=4] {'depth'}, dimensions={0}, use_global_device_ids=true | all-gather | bytes 40960 | tf_op jit(solution)/shard_map/all_gather | solution.py:189
  130.0 9.6 %while.89 = (s32[]{:T(128)}, f32[2,128,128]{2,1,0:T(8,128)S(1)}, f32[2,6,128]{2,1,0:T(8,128)S(1)}, f32[2,6,128]{2,1,0:T(8,128)S(1)}, bf16[2,128,1024]{2,1,0:T(8,...) while((s32[]{:T(128)}, f32[2,128,128]{2,1,0:T(8,128)S(1)}, ...), condition=%wide.region_31.32_spmd, body=%wide.region_21.31_spmd.sunk | while | flops 485672448 | bytes 3947113 | solution.py:198
  142.1 3.7 %all-to-all-start.6 = ((f32[8,1,192]{2,1,0:T(1,128)}), f32[8,1,192]{2,1,0:T(1,128)S(1)}, u32[]{:S(2)}, u32[]{:S(2)}) async-start(f32[8,1,192]{2,1,0:T(1,128)} %reshape.3805), calls=%async_computation.6 | async-start | bytes 16384 | tf_op jit(solution)/shard_map/all_to_all | solution.py:212
  146.5 4.0 %all-to-all-done.6 = f32[8,1,192]{2,1,0:T(1,128)S(1)} async-done(((f32[8,1,192]{2,1,0:T(1,128)}), f32[8,1,192]{2,1,0:T(1,128)S(1)}, u32[]{:S(2)}, u32[]{:S(2)}) %all-to-all-start.6) | async-done | bytes 6176 | tf_op jit(solution)/shard_map/all_to_all | solution.py:212
  150.4 3.3 %all-to-all-start.3 = ((s32[8,1,32]{2,1,0:T(1,128)}), s32[8,1,32]{2,1,0:T(1,128)S(1)}, u32[]{:S(2)}, u32[]{:S(2)}) async-start(s32[8,1,32]{2,1,0:T(1,128)} %all_to_all.40), calls=%async_computation.3 | async-start | bytes 8192 | tf_op jit(solution)/shard_map/all_to_all | solution.py:160
  158.3 3.4 %all-to-all-start.4 = ((f32[8,32,128]{2,1,0:T(8,128)}), f32[8,32,128]{2,1,0:T(8,128)S(1)}, u32[]{:S(2)}, u32[]{:S(2)}) async-start(f32[8,32,128]{2,1,0:T(8,128)} %broadcast_select_fusion.1), calls=%async_computation.4 | async-start | bytes 262144 | tf_op jit(solution)/shard_map/all_to_all | solution.py:211
  163.9 3.3 %all-to-all-done.4 = f32[8,32,128]{2,1,0:T(8,128)S(1)} async-done(((f32[8,32,128]{2,1,0:T(8,128)}), f32[8,32,128]{2,1,0:T(8,128)S(1)}, u32[]{:S(2)}, u32[]{:S(2)}) %all-to-all-start.4) | async-done | bytes 131104 | tf_op jit(solution)/shard_map/all_to_all | solution.py:211
  167.1 3.3 %all-to-all-start.7 = ((f32[8,1,192]{2,1,0:T(1,128)}), f32[8,1,192]{2,1,0:T(1,128)S(1)}, u32[]{:S(2)}, u32[]{:S(2)}) async-start(f32[8,1,192]{2,1,0:T(1,128)} %reshape.3807), calls=%async_computation.7 | async-start | bytes 16384 | tf_op jit(solution)/shard_map/all_to_all | solution.py:162
  175.1 3.4 %all-to-all-start.5 = ((bf16[8,32,128]{2,1,0:T(8,128)(2,1)}), bf16[8,32,128]{2,1,0:T(8,128)(2,1)S(1)}, u32[]{:S(2)}, u32[]{:S(2)}) async-start(bf16[8,32,128]{2,1,0:T(8,128)(2,1)} %bitcast.121), calls=%async_computation.5 | async-start | bytes 131072 | tf_op jit(solution)/shard_map/all_to_all | solution.py:159
  180.6 2.9 all-to-all-done.5
  186.1 5.1 %while.90 = (s32[]{:T(128)}, f32[2,128,1024]{2,1,0:T(8,128)S(1)}, f32[2,1024]{1,0:T(2,128)S(1)}, bf16[2,128,128]{2,1,0:T(8,128)(2,1)S(1)}, f32[2,6,128]{2,1,0:T(8,128)S(1)}, /*index=5*/s32[]{:T(128)}, s32[]{:T(128)}) while((s32[]{:T(128)}, f32[2,128,1024]{2,1,0:T(8,128)S(1)}, f32[2,1024]{1,0:T(2,128)S(1)}, ...), condition=%wide.region_39.40_spmd, body=%wide.region_36.39_spmd.sunk | while | flops 242777600 | bytes 1177693 | solution.py:179
  191.2 13.1 %all-gather.6 = f32[4,2,1024]{2,1,0:T(2,128)S(1)} all-gather(f32[1,2,1024]{2,1,0:T(2,128)S(1)} %bitcast.691), channel_id=4, replica_groups=mesh['tile'=8,'depth'=4] {'depth'}, dimensions={0}, use_global_device_ids=true | all-gather | bytes 40960 | tf_op jit(solution)/shard_map/all_gather | solution.py:180
  206.7 48.4 %all-reduce.9.cloned.1.call-done = f32[2,128,1024]{2,1,0:T(8,128)} async-done(((f32[2,128,1024]{2,1,0:T(8,128)}), f32[2,128,1024]{2,1,0:T(8,128)}) %all-reduce.9.cloned.1.call-update) | async-done | bytes 1048592 | tf_op jit(solution)/shard_map/psum | solution.py:184
  256.6 13.4 %all-gather.7 = f32[4,2,1024]{2,1,0:T(2,128)S(1)} all-gather(f32[1,2,1024]{2,1,0:T(2,128)S(1)} %bitcast.688), channel_id=5, replica_groups=mesh['tile'=8,'depth'=4] {'depth'}, dimensions={0}, use_global_device_ids=true | all-gather | bytes 40960 | tf_op jit(solution)/shard_map/all_gather | solution.py:189
  270.2 9.7 %while.91 = (s32[]{:T(128)}, f32[2,128,128]{2,1,0:T(8,128)S(1)}, f32[2,6,128]{2,1,0:T(8,128)S(1)}, f32[2,6,128]{2,1,0:T(8,128)S(1)}, bf16[2,128,1024]{2,1,0:T(8,...) while((s32[]{:T(128)}, f32[2,128,128]{2,1,0:T(8,128)S(1)}, ...), condition=%wide.region_55.56_spmd, body=%wide.region_45.55_spmd.sunk | while | flops 485672448 | bytes 3947113 | solution.py:198
  283.0 3.7 %all-to-all-start.9 = ((f32[8,1,192]{2,1,0:T(1,128)}), f32[8,1,192]{2,1,0:T(1,128)S(1)}, u32[]{:S(2)}, u32[]{:S(2)}) async-start(f32[8,1,192]{2,1,0:T(1,128)} %reshape.3809), calls=%async_computation.9 | async-start | bytes 16384 | tf_op jit(solution)/shard_map/all_to_all | solution.py:212
  288.4 3.0 all-to-all-done.9
  291.4 3.4 %all-to-all-start.8 = ((f32[8,32,128]{2,1,0:T(8,128)}), f32[8,32,128]{2,1,0:T(8,128)S(1)}, u32[]{:S(2)}, u32[]{:S(2)}) async-start(f32[8,32,128]{2,1,0:T(8,128)} %broadcast_select_fusion), calls=%async_computation.8 | async-start | bytes 262144 | tf_op jit(solution)/shard_map/all_to_all | solution.py:211
  (288 shorter events, 93.3 us)
Async XLA Ops:
  8.8 0.6 copy-start.6
  10.8 0.7 slice-start.2
  11.5 0.7 slice-start.3
  12.3 0.7 copy-start.5
  13.0 7.5 %copy-start.4 = (f32[2,1,5,256]{3,1,2,0:T(1,128)S(1)}, f32[2,1,5,256]{3,1,2,0:T(1,128)}, u32[]{:S(2)}) copy-start(f32[2,1,5,256]{3,1,2,0:T(1,128)} %param.19) | copy-start | bytes 30724
  15.1 5.3 %copy-start.8 = (f32[1,256]{1,0:T(1,128)S(1)}, f32[1,256]{1,0:T(1,128)}, u32[]{:S(2)}) copy-start(f32[1,256]{1,0:T(1,128)} %param.18) | copy-start | bytes 3076
  15.1 9.9 %all-to-all-start = ((s32[8,1,32]{2,1,0:T(1,128)}), s32[8,1,32]{2,1,0:T(1,128)S(1)}, u32[]{:S(2)}, u32[]{:S(2)}) async-start(s32[8,1,32]{2,1,0:T(1,128)} %all_to_all.36), calls=%async_computation | async-start | bytes 8192 | tf_op jit(solution)/shard_map/all_to_all | solution.py:160
  21.9 6.6 %copy-start.3 = (bf16[1,256,128]{2,1,0:T(8,128)(2,1)S(1)}, bf16[1,256,128]{2,1,0:T(8,128)(2,1)}, u32[]{:S(2)}) copy-start(bf16[1,256,128]{2,1,0:T(8,128)(2,1)} %param.17) | copy-start | bytes 196612
  25.1 8.0 %all-to-all-start.2 = ((f32[8,1,192]{2,1,0:T(1,128)}), f32[8,1,192]{2,1,0:T(1,128)S(1)}, u32[]{:S(2)}, u32[]{:S(2)}) async-start(f32[8,1,192]{2,1,0:T(1,128)} %reshape.3803), calls=%async_computation.2 | async-start | bytes 16384 | tf_op jit(solution)/shard_map/all_to_all | solution.py:162
  33.1 8.3 %all-to-all-start.1 = ((bf16[8,32,128]{2,1,0:T(8,128)(2,1)}), bf16[8,32,128]{2,1,0:T(8,128)(2,1)S(1)}, u32[]{:S(2)}, u32[]{:S(2)}) async-start(bf16[8,32,128]{2,1,0:T(8,128)(2,1)} %bitcast.95), calls=%async_computation.1 | async-start | bytes 131072 | tf_op jit(solution)/shard_map/all_to_all | solution.py:159
  36.4 78.5 %all-reduce.7.cloned.1.call-start = ((), (), s32[]{:S(2)}) async-start(), calls=%async_computation.10 | async-start | bytes 2097152 | tf_op jit(solution)/shard_map/psum | solution.py:184
  42.6 0.6 copy-start.2
  43.2 0.8 slice-start.1
  63.8 51.2 %copy-start = (bf16[2,2,128,1024]{3,2,1,0:T(8,128)(2,1)S(1)}, bf16[2,2,128,1024]{3,2,1,0:T(8,128)(2,1)}, u32[]{:S(2)}) copy-start(bf16[2,2,128,1024]{3,2,1,0:T(8,128)(2,1)} %param.21) | copy-start | bytes 3145732
  142.1 8.4 %all-to-all-start.6 = ((f32[8,1,192]{2,1,0:T(1,128)}), f32[8,1,192]{2,1,0:T(1,128)S(1)}, u32[]{:S(2)}, u32[]{:S(2)}) async-start(f32[8,1,192]{2,1,0:T(1,128)} %reshape.3805), calls=%async_computation.6 | async-start | bytes 16384 | tf_op jit(solution)/shard_map/all_to_all | solution.py:212
  150.4 7.9 %all-to-all-start.3 = ((s32[8,1,32]{2,1,0:T(1,128)}), s32[8,1,32]{2,1,0:T(1,128)S(1)}, u32[]{:S(2)}, u32[]{:S(2)}) async-start(s32[8,1,32]{2,1,0:T(1,128)} %all_to_all.40), calls=%async_computation.3 | async-start | bytes 8192 | tf_op jit(solution)/shard_map/all_to_all | solution.py:160
  158.3 8.8 %all-to-all-start.4 = ((f32[8,32,128]{2,1,0:T(8,128)}), f32[8,32,128]{2,1,0:T(8,128)S(1)}, u32[]{:S(2)}, u32[]{:S(2)}) async-start(f32[8,32,128]{2,1,0:T(8,128)} %broadcast_select_fusion.1), calls=%async_computation.4 | async-start | bytes 262144 | tf_op jit(solution)/shard_map/all_to_all | solution.py:211
  167.1 8.0 %all-to-all-start.7 = ((f32[8,1,192]{2,1,0:T(1,128)}), f32[8,1,192]{2,1,0:T(1,128)S(1)}, u32[]{:S(2)}, u32[]{:S(2)}) async-start(f32[8,1,192]{2,1,0:T(1,128)} %reshape.3807), calls=%async_computation.7 | async-start | bytes 16384 | tf_op jit(solution)/shard_map/all_to_all | solution.py:162
  175.1 8.3 %all-to-all-start.5 = ((bf16[8,32,128]{2,1,0:T(8,128)(2,1)}), bf16[8,32,128]{2,1,0:T(8,128)(2,1)S(1)}, u32[]{:S(2)}, u32[]{:S(2)}) async-start(bf16[8,32,128]{2,1,0:T(8,128)(2,1)} %bitcast.121), calls=%async_computation.5 | async-start | bytes 131072 | tf_op jit(solution)/shard_map/all_to_all | solution.py:159
  178.5 76.6 %all-reduce.9.cloned.1.call-start = ((), (), s32[]{:S(2)}) async-start(), calls=%async_computation.11 | async-start | bytes 2097152 | tf_op jit(solution)/shard_map/psum | solution.py:184
  184.6 0.6 copy-start.1
  185.2 0.8 slice-start
  283.0 8.4 %all-to-all-start.9 = ((f32[8,1,192]{2,1,0:T(1,128)}), f32[8,1,192]{2,1,0:T(1,128)S(1)}, u32[]{:S(2)}, u32[]{:S(2)}) async-start(f32[8,1,192]{2,1,0:T(1,128)} %reshape.3809), calls=%async_computation.9 | async-start | bytes 16384 | tf_op jit(solution)/shard_map/all_to_all | solution.py:212
  291.4 8.8 %all-to-all-start.8 = ((f32[8,32,128]{2,1,0:T(8,128)}), f32[8,32,128]{2,1,0:T(8,128)S(1)}, u32[]{:S(2)}, u32[]{:S(2)}) async-start(f32[8,32,128]{2,1,0:T(8,128)} %broadcast_select_fusion), calls=%async_computation.8 | async-start | bytes 262144 | tf_op jit(solution)/shard_map/all_to_all | solution.py:211
  (1 other events, 0.6 us)
Sparse Core Ops, SparseCore 0:
  63.9 51.0 all-reduce.6
  205.7 49.3 all-reduce.8
where the time goes:
time: 310 us; the launch traced here: 308 us
  waiting for transfers between devices  123 us (40%)
  blocking collectives  53.2 us (17%)
  starting transfers between devices  36.2 us (12%)
  local copies, waits for them, and re-layouts  35.9 us (12%)
  matrix products  22.2 us (7%)
  other arithmetic  21.8 us (7%)
  between operations  14.7 us (5%)
    psum x2, waiting for transfers between devices, body(): summed = lax.psum(contrib, 'depth')  97.4 us
    all_gather x2, blocking collectives, body(): all_terms = lax.all_gather(pixel_terms[None], 'depth', axis=0, tiled=True)  26.7 us
    all_gather x2, blocking collectives, body(): all_keeps = lax.all_gather(layer_keeps[None], 'depth', axis=0, tiled=True)  26.5 us
    dot_general x12, matrix products, block_sum(): jnp.einsum('ij,bjp->bip', triangle, blocks, precision=lax.Precision.HIGHEST)  15.4 us
    all_to_all x2, starting transfers between devices, body(): lax.all_to_all(slot_buffer, 'tile', split_axis=0, concat_axis=0, tiled=True)  8.64 us
    all_to_all x2, starting transfers between devices, body(): lax.all_to_all(back_shape, 'tile', split_axis=0, concat_axis=0, tiled=True)  7.32 us
    all_to_all x2, waiting for transfers between devices, body(): lax.all_to_all(back_shape, 'tile', split_axis=0, concat_axis=0, tiled=True)  6.97 us
    unnamed x28, local copies, waits for them, and re-layouts  6.8 us
  transfers between devices with their start and end apart: 12, of which 12 were waited for; matrix products, arithmetic and copies ran while one was open for 8% of the time, Pallas kernels for 0%

commit v1 on v0

--- a/solution.py
+++ b/solution.py
@@ -181,7 +181,7 @@
         earlier_mask = (jnp.arange(layers) < depth_here)[:, None, None]
         ahead = jnp.prod(jnp.where(earlier_mask, all_keeps, 1.0), axis=0)
         contrib = ahead[:, None, :] * composites
-        summed = lax.psum(contrib, "depth")
+        summed = jnp.sum(lax.all_gather(contrib, "depth"), axis=0)
         residual = summed - target[view_index].astype(jnp.float32)
         image_part = lax.dynamic_slice_in_dim(summed, depth_here * pixel_share, pixel_share, 2)
         images.append(image_part.astype(jnp.bfloat16))

time: 310 us -> 382 us (1.23)
  waiting for transfers between devices: 123 us -> 176 us
  other arithmetic: 21.8 us -> 36.5 us
  matrix products: 22.2 us -> 27.6 us
    all_gather x0 -> x2, waiting for transfers between devices: none -> 152 us  [body(): summed = jnp.sum(lax.all_gather(contrib, 'depth'), axis=0)]
    psum x2 -> x0, waiting for transfers between devices: 97.4 us -> none  [body(): summed = lax.psum(contrib, 'depth')]
    reduce_sum x0 -> x2, other arithmetic: none -> 5.42 us  [body(): summed = jnp.sum(lax.all_gather(contrib, 'depth'), axis=0)]
where the time goes in v1:
time: 382 us; the launch traced here: 381 us
  waiting for transfers between devices  176 us (46%)
  blocking collectives  53.4 us (14%)
  other arithmetic  36.5 us (10%)
  starting transfers between devices  36 us (9%)
  local copies, waits for them, and re-layouts  35.5 us (9%)
  matrix products  27.6 us (7%)
  between operations  14.7 us (4%)
    all_gather x2, waiting for transfers between devices, body(): summed = jnp.sum(lax.all_gather(contrib, 'depth'), axis=0)  152 us
    all_gather x2, blocking collectives, body(): all_keeps = lax.all_gather(layer_keeps[None], 'depth', axis=0, tiled=True)  26.9 us
    all_gather x2, blocking collectives, body(): all_terms = lax.all_gather(pixel_terms[None], 'depth', axis=0, tiled=True)  26.5 us
    dot_general x12, matrix products, block_sum(): jnp.einsum('ij,bjp->bip', triangle, blocks, precision=lax.Precision.HIGHEST)  17 us
    all_to_all x2, starting transfers between devices, body(): lax.all_to_all(slot_buffer, 'tile', split_axis=0, concat_axis=0, tiled=True)  8.51 us
    all_to_all x2, waiting for transfers between devices, body(): lax.all_to_all(back_shape, 'tile', split_axis=0, concat_axis=0, tiled=True)  7.93 us
  transfers between devices with their start and end apart: 12, of which 12 were waited for; matrix products, arithmetic and copies ran while one was open for 8% of the time, Pallas kernels for 0%

profile of v1, /device:TPU:0, one launch (start us, length us, event | category | flops | bytes accessed | tf_op | source)
XLA Modules:
  0.0 380.8 jit_solution(17025420022367214789)
XLA Ops:
  12.6 5.2 %all-to-all-start = ((s32[8,1,32]{2,1,0:T(1,128)}), s32[8,1,32]{2,1,0:T(1,128)S(1)}, u32[]{:S(2)}, u32[]{:S(2)}) async-start(s32[8,1,32]{2,1,0:T(1,128)} %all_to_all.36), calls=%async_computation | async-start | bytes 8192 | tf_op jit(solution)/shard_map/all_to_all | solution.py:160
  22.4 3.3 all-to-all-start.2
  30.4 3.4 all-to-all-start.1
  40.1 5.1 %while.88 = (s32[]{:T(128)}, f32[2,128,1024]{2,1,0:T(8,128)S(1)}, f32[2,1024]{1,0:T(2,128)S(1)}, bf16[2,128,128]{2,1,0:T(8,128)(2,1)S(1)}, f32[2,6,128]{2,1,0:T(8,128)S(1)}, /*index=5*/s32[]{:T(128)}, s32[]{:T(128)}) while((s32[]{:T(128)}, f32[2,128,1024]{2,1,0:T(8,128)S(1)}, f32[2,1024]{1,0:T(2,128)S(1)}, ...), condition=%wide.region_11.12_spmd, body=%wide.region_8.11_spmd.sunk | while | flops 242777600 | bytes 1177693 | solution.py:179
  45.2 13.4 %all-gather.6 = f32[4,2,1024]{2,1,0:T(2,128)S(1)} all-gather(f32[1,2,1024]{2,1,0:T(2,128)S(1)} %bitcast.693), channel_id=2, replica_groups=mesh['tile'=8,'depth'=4] {'depth'}, dimensions={0}, use_global_device_ids=true | all-gather | bytes 40960 | tf_op jit(solution)/shard_map/all_gather | solution.py:180
  61.9 77.9 %all-gather.13.cloned.1.call-done = f32[8,128,1024]{2,1,0:T(8,128)} async-done(((f32[2,128,1024]{2,1,0:T(8,128)}), f32[8,128,1024]{2,1,0:T(8,128)}) %all-gather.13.cloned.1.call-update) | async-done | bytes 4194320 | tf_op jit(solution)/shard_map/all_gather | solution.py:184
  143.6 13.3 %all-gather.7 = f32[4,2,1024]{2,1,0:T(2,128)S(1)} all-gather(f32[1,2,1024]{2,1,0:T(2,128)S(1)} %bitcast.692), channel_id=4, replica_groups=mesh['tile'=8,'depth'=4] {'depth'}, dimensions={0}, use_global_device_ids=true | all-gather | bytes 40960 | tf_op jit(solution)/shard_map/all_gather | solution.py:189
  157.2 11.5 %while.89 = (s32[]{:T(128)}, f32[2,128,128]{2,1,0:T(8,128)S(1)}, f32[2,6,128]{2,1,0:T(8,128)S(1)}, f32[2,6,128]{2,1,0:T(8,128)S(1)}, bf16[2,128,1024]{2,1,0:T(8,...) while((s32[]{:T(128)}, f32[2,128,128]{2,1,0:T(8,128)S(1)}, ...), condition=%wide.region_31.32_spmd, body=%wide.region_21.31_spmd.sunk | while | flops 485672448 | bytes 6044293 | solution.py:198
  171.2 3.7 all-to-all-start.6
  175.6 4.0 %all-to-all-done.6 = f32[8,1,192]{2,1,0:T(1,128)S(1)} async-done(((f32[8,1,192]{2,1,0:T(1,128)}), f32[8,1,192]{2,1,0:T(1,128)S(1)}, u32[]{:S(2)}, u32[]{:S(2)}) %all-to-all-start.6) | async-done | bytes 6176 | tf_op jit(solution)/shard_map/all_to_all | solution.py:212
  179.5 3.3 all-to-all-start.3
  184.6 2.8 all-to-all-done.3
  187.4 3.4 all-to-all-start.4
  196.2 3.3 all-to-all-start.7
  204.2 3.4 all-to-all-start.5
  214.4 12.1 %while.90 = (s32[]{:T(128)}, f32[2,128,1024]{2,1,0:T(8,128)S(1)}, f32[2,1024]{1,0:T(2,128)}, bf16[2,128,128]{2,1,0:T(8,128)(2,1)S(1)}, f32[2,6,128]{2,1,0:T(8,128)S(1)}, /*index=5*/s32[]{:T(128)}, s32[]{:T(128)}) while((s32[]{:T(128)}, f32[2,128,1024]{2,1,0:T(8,128)S(1)}, f32[2,1024]{1,0:T(2,128)}, bf16[2,128,128]{2,1,0:T(8,128)(2,1)S(1)}, ...), condition=%wide.region_39.40_spmd, body=%wide.region_36.39_spmd.sunk | while | flops 242777600 | bytes 1206561 | solution.py:179
  226.5 13.6 %all-gather.8 = f32[4,2,1024]{2,1,0:T(2,128)S(1)} all-gather(f32[1,2,1024]{2,1,0:T(2,128)} %bitcast.695), channel_id=5, replica_groups=mesh['tile'=8,'depth'=4] {'depth'}, dimensions={0}, use_global_device_ids=true | all-gather | bytes 40960 | tf_op jit(solution)/shard_map/all_gather | solution.py:180
  246.6 74.1 %all-gather.15.cloned.1.call-done = f32[8,128,1024]{2,1,0:T(8,128)} async-done(((f32[2,128,1024]{2,1,0:T(8,128)}), f32[8,128,1024]{2,1,0:T(8,128)}) %all-gather.15.cloned.1.call-update) | async-done | bytes 4194320 | tf_op jit(solution)/shard_map/all_gather | solution.py:184
  324.4 13.1 %all-gather.9 = f32[4,2,1024]{2,1,0:T(2,128)S(1)} all-gather(f32[1,2,1024]{2,1,0:T(2,128)S(1)} %bitcast.691), channel_id=7, replica_groups=mesh['tile'=8,'depth'=4] {'depth'}, dimensions={0}, use_global_device_ids=true | all-gather | bytes 40960 | tf_op jit(solution)/shard_map/all_gather | solution.py:189
  337.6 2.9 while.93
  340.6 11.6 %while.91 = (s32[]{:T(128)}, f32[2,128,128]{2,1,0:T(8,128)S(1)}, f32[2,6,128]{2,1,0:T(8,128)S(1)}, f32[2,6,128]{2,1,0:T(8,128)S(1)}, bf16[2,128,1024]{2,1,0:T(8,...) while((s32[]{:T(128)}, f32[2,128,128]{2,1,0:T(8,128)S(1)}, ...), condition=%wide.region_55.56_spmd, body=%wide.region_45.55_spmd.sunk | while | flops 485672448 | bytes 6044293 | solution.py:198
  355.4 3.7 all-to-all-start.9
  359.8 4.0 %all-to-all-done.9 = f32[8,1,192]{2,1,0:T(1,128)S(1)} async-done(((f32[8,1,192]{2,1,0:T(1,128)}), f32[8,1,192]{2,1,0:T(1,128)S(1)}, u32[]{:S(2)}, u32[]{:S(2)}) %all-to-all-start.9) | async-done | bytes 6176 | tf_op jit(solution)/shard_map/all_to_all | solution.py:212
  363.8 3.4 all-to-all-start.8
  (330 shorter events, 113.0 us)
Async XLA Ops:
  10.5 190.5 %copy-start.18 = (s32[256,1]{0,1:T(1,128)}, s32[256,1]{0,1:T(1,128)S(1)}, u32[]{:S(2)}) copy-start(s32[256,1]{0,1:T(1,128)S(1)} %get-tuple-element.807) | copy-start | bytes 3076
  12.6 9.8 %all-to-all-start = ((s32[8,1,32]{2,1,0:T(1,128)}), s32[8,1,32]{2,1,0:T(1,128)S(1)}, u32[]{:S(2)}, u32[]{:S(2)}) async-start(s32[8,1,32]{2,1,0:T(1,128)} %all_to_all.36), calls=%async_computation | async-start | bytes 8192 | tf_op jit(solution)/shard_map/all_to_all | solution.py:160
  22.4 8.0 %all-to-all-start.2 = ((f32[8,1,192]{2,1,0:T(1,128)}), f32[8,1,192]{2,1,0:T(1,128)S(1)}, u32[]{:S(2)}, u32[]{:S(2)}) async-start(f32[8,1,192]{2,1,0:T(1,128)} %reshape.3805), calls=%async_computation.2 | async-start | bytes 16384 | tf_op jit(solution)/shard_map/all_to_all | solution.py:162
  25.8 32.8 %copy-start.21 = (pred[4]{0:T(512)(128)(4,1)}, pred[4]{0:T(512)(128)(4,1)S(1)}, u32[]{:S(2)}) copy-start(pred[4]{0:T(512)(128)(4,1)S(1)} %iota_compare_fusion.16) | copy-start | bytes 16
  30.4 8.3 %all-to-all-start.1 = ((bf16[8,32,128]{2,1,0:T(8,128)(2,1)}), bf16[8,32,128]{2,1,0:T(8,128)(2,1)S(1)}, u32[]{:S(2)}, u32[]{:S(2)}) async-start(bf16[8,32,128]{2,1,0:T(8,128)(2,1)} %bitcast.95), calls=%async_computation.1 | async-start | bytes 131072 | tf_op jit(solution)/shard_map/all_to_all | solution.py:159
  33.8 106.1 %all-gather.13.cloned.1.call-start = ((), (), s32[]{:S(2)}) async-start(), calls=%async_computation.10 | async-start | bytes 5242880 | tf_op jit(solution)/shard_map/all_gather | solution.py:184
  58.7 83.9 %copy-start = (bf16[2,2,128,1024]{3,2,1,0:T(8,128)(2,1)S(1)}, bf16[2,2,128,1024]{3,2,1,0:T(8,128)(2,1)}, u32[]{:S(2)}) copy-start(bf16[2,2,128,1024]{3,2,1,0:T(8,128)(2,1)} %param.21) | copy-start | bytes 3145732
  168.7 22.1 %copy-start.20 = (f32[1,256]{1,0:T(1,128)S(1)}, f32[1,256]{1,0:T(1,128)}, u32[]{:S(2)}) copy-start(f32[1,256]{1,0:T(1,128)} %param.18) | copy-start | bytes 3076
  168.7 32.3 %copy-start.1 = (bf16[1,256,128]{2,1,0:T(8,128)(2,1)S(1)}, bf16[1,256,128]{2,1,0:T(8,128)(2,1)}, u32[]{:S(2)}) copy-start(bf16[1,256,128]{2,1,0:T(8,128)(2,1)} %param.17) | copy-start | bytes 196612
  171.2 8.4 %all-to-all-start.6 = ((f32[8,1,192]{2,1,0:T(1,128)}), f32[8,1,192]{2,1,0:T(1,128)S(1)}, u32[]{:S(2)}, u32[]{:S(2)}) async-start(f32[8,1,192]{2,1,0:T(1,128)} %reshape.3807), calls=%async_computation.6 | async-start | bytes 16384 | tf_op jit(solution)/shard_map/all_to_all | solution.py:212
  179.5 7.9 %all-to-all-start.3 = ((s32[8,1,32]{2,1,0:T(1,128)}), s32[8,1,32]{2,1,0:T(1,128)S(1)}, u32[]{:S(2)}, u32[]{:S(2)}) async-start(s32[8,1,32]{2,1,0:T(1,128)} %all_to_all.40), calls=%async_computation.3 | async-start | bytes 8192 | tf_op jit(solution)/shard_map/all_to_all | solution.py:160
  187.4 25.1 %copy-start.10 = (s32[8,1,32]{2,1,0:T(1,128)}, s32[8,1,32]{2,1,0:T(1,128)S(1)}, u32[]{:S(2)}) copy-start(s32[8,1,32]{2,1,0:T(1,128)S(1)} %all-to-all-done.3) | copy-start | bytes 3076
  187.4 8.8 %all-to-all-start.4 = ((f32[8,32,128]{2,1,0:T(8,128)}), f32[8,32,128]{2,1,0:T(8,128)S(1)}, u32[]{:S(2)}, u32[]{:S(2)}) async-start(f32[8,32,128]{2,1,0:T(8,128)} %broadcast_select_fusion.1), calls=%async_computation.4 | async-start | bytes 262144 | tf_op jit(solution)/shard_map/all_to_all | solution.py:211
  196.2 8.0 %all-to-all-start.7 = ((f32[8,1,192]{2,1,0:T(1,128)}), f32[8,1,192]{2,1,0:T(1,128)S(1)}, u32[]{:S(2)}, u32[]{:S(2)}) async-start(f32[8,1,192]{2,1,0:T(1,128)} %reshape.3809), calls=%async_computation.7 | async-start | bytes 16384 | tf_op jit(solution)/shard_map/all_to_all | solution.py:162
  204.2 8.3 %all-to-all-start.5 = ((bf16[8,32,128]{2,1,0:T(8,128)(2,1)}), bf16[8,32,128]{2,1,0:T(8,128)(2,1)S(1)}, u32[]{:S(2)}, u32[]{:S(2)}) async-start(bf16[8,32,128]{2,1,0:T(8,128)(2,1)} %bitcast.122), calls=%async_computation.5 | async-start | bytes 131072 | tf_op jit(solution)/shard_map/all_to_all | solution.py:159
  207.6 113.1 %all-gather.15.cloned.1.call-start = ((), (), s32[]{:S(2)}) async-start(), calls=%async_computation.11 | async-start | bytes 5242880 | tf_op jit(solution)/shard_map/all_gather | solution.py:184
  246.5 76.9 %copy-start.8 = (f32[2,1024]{1,0:T(2,128)S(1)}, f32[2,1024]{1,0:T(2,128)}, u32[]{:S(2)}) copy-start(f32[2,1024]{1,0:T(2,128)} %copy-done.7) | copy-start | bytes 24580
  320.6 17.0 %copy-start.6 = (f32[2,1024]{1,0:T(2,128)S(1)}, f32[2,1024]{1,0:T(2,128)}, u32[]{:S(2)}) copy-start(f32[2,1024]{1,0:T(2,128)} %custom-call.1) | copy-start | bytes 24580
  340.6 11.8 %copy-start.17 = (s32[1024]{0:T(1024)S(1)}, s32[1024]{0:T(1024)}, u32[]{:S(2)}) copy-start(s32[1024]{0:T(1024)} %pad_clamp_fusion.1) | copy-start | bytes 12292
  340.6 18.5 %copy-start.2 = (bf16[1,2,128,256]{3,2,1,0:T(8,128)(2,1)S(1)}, bf16[1,2,128,256]{3,2,1,0:T(8,128)(2,1)}, u32[]{:S(2)}) copy-start(bf16[1,2,128,256]{3,2,1,0:T(8,128)(2,1)} %fusion.228) | copy-start | bytes 393220
  346.4 2.9 copy-start.3
  352.2 17.4 %copy-start.19 = (f32[1,256]{1,0:T(1,128)S(1)}, f32[1,256]{1,0:T(1,128)}, u32[]{:S(2)}) copy-start(f32[1,256]{1,0:T(1,128)} %get-tuple-element.753) | copy-start | bytes 3076
  355.4 8.4 %all-to-all-start.9 = ((f32[8,1,192]{2,1,0:T(1,128)}), f32[8,1,192]{2,1,0:T(1,128)S(1)}, u32[]{:S(2)}, u32[]{:S(2)}) async-start(f32[8,1,192]{2,1,0:T(1,128)} %reshape.3811), calls=%async_computation.9 | async-start | bytes 16384 | tf_op jit(solution)/shard_map/all_to_all | solution.py:212
  363.8 8.8 %all-to-all-start.8 = ((f32[8,32,128]{2,1,0:T(8,128)}), f32[8,32,128]{2,1,0:T(8,128)S(1)}, u32[]{:S(2)}, u32[]{:S(2)}) async-start(f32[8,32,128]{2,1,0:T(8,128)} %broadcast_select_fusion), calls=%async_computation.8 | async-start | bytes 262144 | tf_op jit(solution)/shard_map/all_to_all | solution.py:211
  (19 other events, 24.1 us)
Sparse Core Ops, SparseCore 0:
  59.9 79.8 all-gather.12
  243.3 77.3 all-gather.14
